TPU v7x, 32 devices: a whole 2x2x4 slice. The times are simulated.
32 devices in a mesh: dp: 8 (over z, y), ctx: 4 (over x, core).
Axes of the slice: x: 2, y: 2, z: 4, core: 2. Of those that a mesh axis runs over, the one named last changes fastest.
Arguments:
- projected: bfloat16 [8, 512, 3, 4096], P('dp', 'ctx'), may hold values from -6 to 6
- short_taps: float32 [3, 3, 4096], P(None, None, 'ctx'), may hold values from -3 to 3
- long_filter: bfloat16 [512, 4096], P('dp', 'ctx'), may hold values from -1.1 to 1.1
- skip_gain: float32 [4096], P('ctx'), may hold values from -4 to 4
Outputs:
- mixed: bfloat16 [8, 512, 4096], P('dp', 'ctx')
All inputs are finite; a program needn't handle non-finite values.
Results may differ from a plain program's by a relative error of at most 0.012.
Values may be sent and summed in bfloat16 or wider, within the bound.
A program may use at most 64 MiB of HBM per device.

v0:
```python
import math

import jax
import jax.numpy as jnp
from jax import lax
from jax.sharding import PartitionSpec as P

RADIX = 64


HIGH = lax.Precision.HIGHEST


def causal_short(extended, taps, kernel_size):
    row_count = extended.shape[0] - (kernel_size - 1)
    widened = extended.astype(jnp.float32)
    summed = jnp.zeros((row_count,) + widened.shape[1:], jnp.float32)
    for tap_index in range(kernel_size):
        offset = kernel_size - 1 - tap_index
        summed = summed + taps[tap_index] * widened[offset : offset + row_count]
    return (summed[:, 0].astype(jnp.bfloat16), (summed[:, 1] * summed[:, 2]).astype(jnp.bfloat16))


def dft_tables(length, radix_size):
    outer_size = 2 * length // radix_size
    total_size = outer_size * radix_size
    outer_range = jnp.arange(outer_size, dtype=jnp.int32)
    inner_range = jnp.arange(radix_size, dtype=jnp.int32)
    angle_one = (
        2.0
        * math.pi
        / outer_size
        * (outer_range[:, None] * outer_range[None, :] % outer_size).astype(jnp.float32)
    )
    angle_twist = (
        2.0
        * math.pi
        / total_size
        * (outer_range[:, None] * inner_range[None, :] % total_size).astype(jnp.float32)
    )
    angle_two = (
        2.0
        * math.pi
        / radix_size
        * (inner_range[:, None] * inner_range[None, :] % radix_size).astype(jnp.float32)
    )
    twist_cos = jnp.cos(angle_twist)[:, :, None]
    twist_sin = jnp.sin(angle_twist)[:, :, None]
    return (
        jnp.cos(angle_one),
        jnp.sin(angle_one),
        twist_cos,
        twist_sin,
        jnp.cos(angle_two),
        jnp.sin(angle_two),
    )


def forward_dft(signal, tables, radix_size):
    cos_one, sin_one, twist_cos, twist_sin, cos_two, sin_two = tables
    outer_size = cos_one.shape[0]
    half_size = outer_size // 2
    block_width = signal.shape[1]
    shaped = signal.reshape(half_size, radix_size * block_width)
    first_re = jnp.dot(cos_one[:, :half_size], shaped, precision=HIGH).reshape(
        outer_size, radix_size, block_width
    )
    first_im = -jnp.dot(sin_one[:, :half_size], shaped, precision=HIGH).reshape(
        outer_size, radix_size, block_width
    )
    second_re = first_re * twist_cos + first_im * twist_sin
    second_im = first_im * twist_cos - first_re * twist_sin
    spec_re = jnp.einsum("amc,mb->abc", second_re, cos_two, precision=HIGH) + jnp.einsum(
        "amc,mb->abc", second_im, sin_two, precision=HIGH
    )
    spec_im = jnp.einsum("amc,mb->abc", second_im, cos_two, precision=HIGH) - jnp.einsum(
        "amc,mb->abc", second_re, sin_two, precision=HIGH
    )
    return (spec_re, spec_im)


def inverse_dft(spec_re, spec_im, tables, radix_size):
    cos_one, sin_one, twist_cos, twist_sin, cos_two, sin_two = tables
    outer_size = cos_one.shape[0]
    half_size = outer_size // 2
    block_width = spec_re.shape[2]
    back_re = jnp.einsum("abc,mb->amc", spec_re, cos_two, precision=HIGH) - jnp.einsum(
        "abc,mb->amc", spec_im, sin_two, precision=HIGH
    )
    back_im = jnp.einsum("abc,mb->amc", spec_re, sin_two, precision=HIGH) + jnp.einsum(
        "abc,mb->amc", spec_im, cos_two, precision=HIGH
    )
    turned_re = (back_re * twist_cos - back_im * twist_sin).reshape(
        outer_size, radix_size * block_width
    )
    turned_im = (back_re * twist_sin + back_im * twist_cos).reshape(
        outer_size, radix_size * block_width
    )
    result = jnp.dot(cos_one[:half_size], turned_re, precision=HIGH) - jnp.dot(
        sin_one[:half_size], turned_im, precision=HIGH
    )
    return result.reshape(half_size * radix_size, block_width) / (outer_size * radix_size)


def long_convolve(gated_slab, filter_slab):
    length, channels = gated_slab.shape
    block_width = min(128, channels)
    tables = dft_tables(length, RADIX)

    def one_block(block_index, output):
        offset = block_index * block_width
        signal = lax.dynamic_slice_in_dim(gated_slab, offset, block_width, 1).astype(jnp.float32)
        kernel_block = lax.dynamic_slice_in_dim(filter_slab, offset, block_width, 1).astype(
            jnp.float32
        )
        sig_re, sig_im = forward_dft(signal, tables, RADIX)
        ker_re, ker_im = forward_dft(kernel_block, tables, RADIX)
        prod_re = sig_re * ker_re - sig_im * ker_im
        prod_im = sig_re * ker_im + sig_im * ker_re
        result = inverse_dft(prod_re, prod_im, tables, RADIX)
        return lax.dynamic_update_slice_in_dim(output, result, offset, 1)

    return lax.fori_loop(
        0, channels // block_width, one_block, jnp.zeros((length, channels), jnp.float32)
    )


def make_response(gated_slab, filter_slab, skip_gain):
    long_part = long_convolve(gated_slab, filter_slab)
    return (long_part + skip_gain * gated_slab.astype(jnp.float32)).astype(jnp.bfloat16)


def combine_rows(query_part, response_part):
    return (query_part.astype(jnp.float32) * response_part.astype(jnp.float32)).astype(jnp.bfloat16)


def on_device(projected, short_taps, long_filter, skip_gain):
    kernel_size = short_taps.shape[0]
    tok_rows = projected[0]
    filter_slab = lax.all_gather(long_filter, "dp", axis=0, tiled=True)
    stream_slab = lax.all_to_all(tok_rows, "ctx", split_axis=2, concat_axis=0, tiled=True)
    extended = jnp.pad(stream_slab, ((kernel_size - 1, 0), (0, 0), (0, 0)))
    query_slab, gated_slab = causal_short(extended, short_taps, kernel_size)
    response_slab = make_response(gated_slab, filter_slab, skip_gain)
    mixed = lax.all_to_all(
        combine_rows(query_slab, response_slab), "ctx", split_axis=0, concat_axis=1, tiled=True
    )
    return mixed[None]


def solution(mesh):
    return jax.shard_map(
        on_device,
        mesh=mesh,
        in_specs=(P("dp", "ctx", None, None), P(None, None, "ctx"), P("dp", "ctx"), P("ctx")),
        out_specs=P("dp", "ctx", None),
        check_vma=False,
    )
```

profile of v0, /device:TPU:0, one launch (start us, length us, event | category | flops | bytes accessed | tf_op | source)
XLA Modules:
  0.0 225.1 jit_solution(1443863807638157853)
XLA Ops:
  6.5 7.2 %copy.33 = bf16[1,128,3,4096]{1,2,3,0:T(4,128)(2,1)} copy(bf16[1,128,3,4096]{3,1,2,0:T(8,128)(2,1)} %param.6) | data formatting | bytes 6291456 | tf_op args[0]
  13.8 5.0 %all-to-all-start = ((bf16[128,3,4096]{0,1,2:T(4,128)(2,1)}), bf16[128,3,4096]{0,1,2:T(4,128)(2,1)}, u32[]{:S(2)}, u32[]{:S(2)}) async-start(bf16[128,3,4096]{0,1,2:T(4,128)(2,1)} %bitcast.224), calls=%async_computation | async-start | bytes 8388608 | tf_op jit(solution)/shard_map/all_to_all | solution.py:141
  19.6 48.0 %all-to-all-done = bf16[128,3,4096]{0,1,2:T(4,128)(2,1)} async-done(((bf16[128,3,4096]{0,1,2:T(4,128)(2,1)}), bf16[128,3,4096]{0,1,2:T(4,128)(2,1)}, u32[]{:S(2)}, u32[]{:S(2)}) %all-to-all-start) | async-done | bytes 3145760 | tf_op jit(solution)/shard_map/all_to_all | solution.py:141
  67.6 5.5 %copy.34 = bf16[4,128,3,1024]{3,1,0,2:T(8,128)(2,1)S(1)} copy(bf16[4,128,3,1024]{1,2,3,0:T(4,128)(2,1)} %bitcast.3) | data formatting | bytes 6291456 | tf_op jit(solution)/shard_map/all_to_all | solution.py:141
  73.1 0.9 pad_convert_fusion
  74.0 1.9 fusion.123
  75.9 2.6 %copy-done = f32[512,3,1024]{2,0,1:T(8,128)} copy-done((f32[512,3,1024]{2,0,1:T(8,128)}, f32[512,3,1024]{2,0,1:T(8,128)S(1)}, u32[]{:S(2)}) %copy-start) | copy-done | bytes 6291480
  78.6 1.3 fusion.128
  80.1 115.5 %while.15 = (s32[]{:T(128)}, f32[512,1024]{1,0:T(8,128)S(1)}, bf16[512,1024]{1,0:T(8,128)(2,1)}, f32[16,16]{1,0:T(8,128)S(1)}, f32[16,16]{1,0:T(8,128)S(1)}, /*i...) while((s32[]{:T(128)}, f32[512,1024]{1,0:T(8,128)S(1)}, ...), condition=%wide.region_1.2_spmd.clone.clone, body=%wide.region_0.1_spmd.clone.clone.sunk | while | flops 1288484864 | bytes 33853592 | solution.py:123
  80.3 1.0 constant_dynamic-slice_fusion.3
  89.2 0.9 multiply_add_fusion.4
  92.3 0.9 multiply_add_fusion.5
  94.7 1.0 constant_dynamic-slice_fusion.3
  106.7 0.9 multiply_add_fusion.5
  109.1 1.0 constant_dynamic-slice_fusion.3
  121.1 0.9 multiply_add_fusion.5
  123.5 1.0 constant_dynamic-slice_fusion.3
  138.0 1.0 constant_dynamic-slice_fusion.3
  152.4 1.0 constant_dynamic-slice_fusion.3
  166.8 1.0 constant_dynamic-slice_fusion.3
  181.2 1.0 constant_dynamic-slice_fusion.3
  195.6 3.8 %fusion.126 = bf16[512,1024]{1,0:T(8,128)(2,1)S(1)} fusion(f32[512,1024]{1,0:T(8,128)S(1)} %get-tuple-element.246, f32[512,3,1024]{2,0,1:T(8,128)} %copy-done, f32[1024]{0:T(1024)S(1)} %copy-done.2), kind=kLoop, calls=%fused_computation.151 | loop fusion | flops 5242880 | bytes 8392704 | tf_op jit(solution)/shard_map/convert_element_type | solution.py:134
  199.4 16.9 %all_to_all.34 = bf16[4,128,1024]{2,1,0:T(8,128)(2,1)S(1)} all-to-all(bf16[4,128,1024]{2,1,0:T(8,128)(2,1)S(1)} %bitcast.227), channel_id=1, replica_groups=mesh['dp'=8,'ctx'=4] {'ctx'}, dimensions={0} | all-to-all | bytes 2097152 | tf_op jit(solution)/shard_map/all_to_all | solution.py:145
  217.0 1.3 copy.36
  (232 shorter events, 103.5 us)
Async XLA Ops:
  13.8 5.8 %copy-start.1 = (f32[3,3,1024]{2,1,0:T(4,128)S(1)}, f32[3,3,1024]{2,1,0:T(4,128)}, u32[]{:S(2)}) copy-start(f32[3,3,1024]{2,1,0:T(4,128)} %param.7) | copy-start | bytes 110596
  13.8 53.8 %all-to-all-start = ((bf16[128,3,4096]{0,1,2:T(4,128)(2,1)}), bf16[128,3,4096]{0,1,2:T(4,128)(2,1)}, u32[]{:S(2)}, u32[]{:S(2)}) async-start(bf16[128,3,4096]{0,1,2:T(4,128)(2,1)} %bitcast.224), calls=%async_computation | async-start | bytes 8388608 | tf_op jit(solution)/shard_map/all_to_all | solution.py:141
  18.7 61.1 %all-gather.2.cloned.1.call-start = ((), (), s32[]{:S(2)}) async-start(), calls=%async_computation.2 | async-start | bytes 1179648 | tf_op jit(solution)/shard_map/all_gather | solution.py:140
  75.9 2.7 %copy-start = (f32[512,3,1024]{2,0,1:T(8,128)}, f32[512,3,1024]{2,0,1:T(8,128)S(1)}, u32[]{:S(2)}) copy-start(f32[512,3,1024]{2,0,1:T(8,128)S(1)} %fusion.123) | copy-start | bytes 18874372
  80.1 115.5 %copy-start.2 = (f32[1024]{0:T(1024)S(1)}, f32[1024]{0:T(1024)}, u32[]{:S(2)}) copy-start(f32[1024]{0:T(1024)} %param.9) | copy-start | bytes 12292
Sparse Core Ops, SparseCore 0:
  21.7 43.2 all-gather.1
where the time goes:
time: 226 us; the launch traced here: 225 us
  matrix products  96.6 us (43%)
  waiting for transfers between devices  48.7 us (22%)
  local copies, waits for them, and re-layouts  30.4 us (13%)
  blocking collectives  16.9 us (7%)
  between operations  13.5 us (6%)
  other arithmetic  11.9 us (5%)
  starting transfers between devices  5.02 us (2%)
    all_to_all x1, waiting for transfers between devices, on_device(): lax.all_to_all(tok_rows, 'ctx', split_axis=2, concat_axis=0, tiled=True)  48 us
    all_to_all x1, blocking collectives, on_device(): lax.all_to_all(combine_rows(query_slab, response_slab), 'ctx', split_axis...  16.9 us
    dot_general x16, matrix products, forward_dft(): jnp.einsum('amc,mb->abc', second_re, sin_two, precision=HIGH)  13.3 us
    dot_general x16, matrix products, forward_dft(): jnp.einsum('amc,mb->abc', second_im, sin_two, precision=HIGH)  12.1 us
    dot_general x16, matrix products, forward_dft(): jnp.einsum('amc,mb->abc', second_re, cos_two, precision=HIGH)  12 us
    dot_general x16, matrix products, forward_dft(): jnp.einsum('amc,mb->abc', second_im, cos_two, precision=HIGH)  12 us
    unnamed x7, local copies, waits for them, and re-layouts  9.88 us
    dynamic_slice x8, local copies, waits for them, and re-layouts, one_block(): lax.dynamic_slice_in_dim(filter_slab, offset, block_width, 1)  7.97 us
  transfers between devices with their start and end apart: 2, of which 1 were waited for; matrix products, arithmetic and copies ran while one was open for 4% of the time, Pallas kernels for 0%

commit v1 on v0

--- a/solution.py
+++ b/solution.py
@@ -2,6 +2,7 @@
 
 import jax
 import jax.numpy as jnp
+import numpy as np
 from jax import lax
 from jax.sharding import PartitionSpec as P
 
@@ -102,7 +103,7 @@
     return result.reshape(half_size * radix_size, block_width) / (outer_size * radix_size)
 
 
-def long_convolve(gated_slab, filter_slab):
+def long_convolve_blocked(gated_slab, filter_slab):
     length, channels = gated_slab.shape
     block_width = min(128, channels)
     tables = dft_tables(length, RADIX)
@@ -125,6 +126,27 @@
     )
 
 
+def long_convolve(gated_slab, filter_slab):
+    length = gated_slab.shape[0]
+    if length > 1024:
+        return long_convolve_blocked(gated_slab, filter_slab)
+    forward, backward = quarter_tables(length)
+    sig = jnp.dot(forward, gated_slab, preferred_element_type=jnp.float32)
+    ker = jnp.dot(forward, filter_slab, preferred_element_type=jnp.float32)
+    sig_cos, sig_sin, ker_cos, ker_sin = sig[:length], sig[length:], ker[:length], ker[length:]
+    prod = jnp.concatenate(
+        [sig_cos * ker_cos - sig_sin * ker_sin, sig_cos * ker_sin + sig_sin * ker_cos]
+    ).astype(jnp.bfloat16)
+    return jnp.dot(backward, prod, preferred_element_type=jnp.float32)
+
+
+def quarter_tables(length):
+    steps = (4 * np.arange(length)[:, None] + 1) * np.arange(length)[None, :] % (4 * length)
+    angles = steps * (2.0 * math.pi / (4 * length))
+    table = np.concatenate([np.cos(angles), np.sin(angles)])
+    return (jnp.asarray(table, jnp.bfloat16), jnp.asarray(table.T / length, jnp.bfloat16))
+
+
 def make_response(gated_slab, filter_slab, skip_gain):
     long_part = long_convolve(gated_slab, filter_slab)
     return (long_part + skip_gain * gated_slab.astype(jnp.float32)).astype(jnp.bfloat16)
@@ -136,16 +158,18 @@
 
 def on_device(projected, short_taps, long_filter, skip_gain):
     kernel_size = short_taps.shape[0]
-    tok_rows = projected[0]
+    ctx_size = lax.axis_size("ctx")
+    rows = projected[0]
     filter_slab = lax.all_gather(long_filter, "dp", axis=0, tiled=True)
-    stream_slab = lax.all_to_all(tok_rows, "ctx", split_axis=2, concat_axis=0, tiled=True)
-    extended = jnp.pad(stream_slab, ((kernel_size - 1, 0), (0, 0), (0, 0)))
-    query_slab, gated_slab = causal_short(extended, short_taps, kernel_size)
+    all_taps = lax.all_gather(short_taps, "ctx", axis=2, tiled=True)
+    halo = lax.ppermute(
+        rows[-(kernel_size - 1) :], "ctx", [(i, i + 1) for i in range(ctx_size - 1)]
+    )
+    queries, gated = causal_short(jnp.concatenate([halo, rows]), all_taps, kernel_size)
+    gated_slab = lax.all_to_all(gated, "ctx", split_axis=1, concat_axis=0, tiled=True)
     response_slab = make_response(gated_slab, filter_slab, skip_gain)
-    mixed = lax.all_to_all(
-        combine_rows(query_slab, response_slab), "ctx", split_axis=0, concat_axis=1, tiled=True
-    )
-    return mixed[None]
+    response = lax.all_to_all(response_slab, "ctx", split_axis=0, concat_axis=1, tiled=True)
+    return combine_rows(queries, response)[None]
 
 
 def solution(mesh):

time: 226 us -> 98.7 us (0.44)
  matrix products: 96.6 us -> 9.08 us
  waiting for transfers between devices: 48.7 us -> 0.02 us
  blocking collectives: 16.9 us -> 40.9 us
  local copies, waits for them, and re-layouts: 30.4 us -> 15.1 us
  other arithmetic: 11.9 us -> 17.3 us
  starting transfers between devices: 5.02 us -> 2.36 us
    dot_general x144 -> x4, matrix products: 96.6 us -> 9.08 us  [the longest x1 4.5 us: long_convolve(): sig = jnp.dot(forward, gated_slab, preferred_element_type=jnp.float32)]
    all_to_all x1 -> x0, waiting for transfers between devices: 48 us -> none  [on_device(): lax.all_to_all(tok_rows, 'ctx', split_axis=2, concat_axis=0, tiled=True)]
    all_to_all x1 -> x2, blocking collectives: 16.9 us -> 33.8 us  [the longest x1 16.9 us: on_device(): lax.all_to_all(response_slab, 'ctx', split_axis=0, concat_axis=1, tiled=T...]
    dynamic_slice x8 -> x0, local copies, waits for them, and re-layouts: 7.97 us -> none  [one_block(): lax.dynamic_slice_in_dim(filter_slab, offset, block_width, 1)]
    add x1, other arithmetic: 1.89 us -> 9.39 us  [causal_short(): summed = summed + taps[tap_index] * widened[offset:offset + row_count]]
    all_gather x0 -> x1, blocking collectives: none -> 7.11 us  [on_device(): all_taps = lax.all_gather(short_taps, 'ctx', axis=2, tiled=True)]
    all_to_all x2 -> x1, local copies, waits for them, and re-layouts: 6.16 us -> 0.81 us  [on_device(): lax.all_to_all(gated, 'ctx', split_axis=1, concat_axis=0, tiled=True)]
    all_to_all x1 -> x0, starting transfers between devices: 4.98 us -> none  [on_device(): lax.all_to_all(tok_rows, 'ctx', split_axis=2, concat_axis=0, tiled=True)]
  transfers between devices with their start and end apart: 2 -> 2, of which waited for: 1 -> 0; matrix products, arithmetic and copies ran while one was open for 4% -> 27% of each run, Pallas kernels for 0% -> 0%
where the time goes in v1:
time: 98.7 us; the launch traced here: 98.3 us
  blocking collectives  40.9 us (41%)
  other arithmetic  17.3 us (18%)
  local copies, waits for them, and re-layouts  15.1 us (15%)
  between operations  13.5 us (14%)
  matrix products  9.08 us (9%)
  starting transfers between devices  2.36 us (2%)
    all_to_all x1, blocking collectives, on_device(): lax.all_to_all(response_slab, 'ctx', split_axis=0, concat_axis=1, tiled=T...  16.9 us
    all_to_all x1, blocking collectives, on_device(): lax.all_to_all(gated, 'ctx', split_axis=1, concat_axis=0, tiled=True)  16.9 us
    add x1, other arithmetic, causal_short(): summed = summed + taps[tap_index] * widened[offset:offset + row_count]  9.39 us
    all_gather x1, blocking collectives, on_device(): all_taps = lax.all_gather(short_taps, 'ctx', axis=2, tiled=True)  7.11 us
    unnamed x11, local copies, waits for them, and re-layouts  6.44 us
    dot_general x1, matrix products, long_convolve(): sig = jnp.dot(forward, gated_slab, preferred_element_type=jnp.float32)  4.5 us
    convert_element_type x1, other arithmetic, causal_short(): widened = extended.astype(jnp.float32)  4.08 us
    dot_general x1, matrix products, long_convolve(): ker = jnp.dot(forward, filter_slab, preferred_element_type=jnp.float32)  2.94 us
  transfers between devices with their start and end apart: 2, of which 0 were waited for; matrix products, arithmetic and copies ran while one was open for 27% of the time, Pallas kernels for 0%

profile of v1, /device:TPU:0, one launch (start us, length us, event | category | flops | bytes accessed | tf_op | source)
XLA Modules:
  0.0 98.3 jit_solution(9374394444664084530)
XLA Ops:
  6.5 1.0 slice_bitcast_fusion.3
  7.5 2.4 %collective-permute-start = (bf16[2,3,4096]{2,0,1:T(2,128)(2,1)S(1)}, bf16[2,3,4096]{2,0,1:T(2,128)(2,1)S(1)}, u32[]{:S(2)}, u32[]{:S(2)}) collective-permute-start(bf16[2,3,4096]{2,0,1:T(2,128)(2,1)S(1)} %slice_bitcast_fusion.3), channel_id=1, source_target_pairs={{0,1},{1,2},{2,3},{4,5},{5,6},{6,7},{8,9},{9,10},{10,11},{12,13},{... | collective-permute-start | bytes 147464 | tf_op jit(solution)/shard_map/ppermute | solution.py:165
  9.9 7.1 %all_gather.6 = f32[3,3,4096]{2,1,0:T(4,128)S(1)} all-gather(f32[3,3,1024]{2,1,0:T(4,128)} %param.7), channel_id=1, replica_groups=mesh['dp'=8,'ctx'=4] {'ctx'}, dimensions={2}, use_global_device_ids=true | all-gather | bytes 184320 | tf_op jit(solution)/shard_map/all_gather | solution.py:164
  17.1 3.5 %copy.19 = bf16[1,128,3,4096]{1,3,2,0:T(8,128)(2,1)S(1)} copy(bf16[1,128,3,4096]{3,1,2,0:T(8,128)(2,1)} %param.6) | data formatting | bytes 6291456 | tf_op args[0]
  20.6 2.8 %copy.20 = bf16[2,3,4096]{0,2,1:T(8,128)(2,1)} copy(bf16[2,3,4096]{2,0,1:T(2,128)(2,1)S(1)} %collective-permute-done) | data formatting | bytes 98304 | tf_op jit(solution)/shard_map/ppermute | solution.py:165
  23.4 4.1 %maximum_convert_fusion = f32[130,3,4096]{0,2,1:T(8,128)S(1)} fusion(bf16[128,3,4096]{0,2,1:T(8,128)(2,1)S(1)} %bitcast.36, bf16[2,3,4096]{0,2,1:T(8,128)(2,1)} %copy.20), kind=kLoop, calls=%fused_computation.5 | loop fusion | flops 6389760 | bytes 9584640 | tf_op jit(solution)/shard_map/convert_element_type | solution.py:17
  27.5 9.4 %fusion = f32[128,3,4096]{0,2,1:T(8,128)S(1)} fusion(f32[130,3,4096]{0,2,1:T(8,128)S(1)} %maximum_convert_fusion, f32[3,4096]{1,0:T(4,128)S(1)} %get-tuple-element.6, f32[3,4096]{1,0:T(4,128)S(1)} %get-tuple-element.7, f32[3,4096]{1,0:T(4,128)S(1)} %get-tuple-element.5), kind=kLoop, calls=%fused_computation.1 | loop fusion | flops 7864320 | bytes 25313280 | tf_op jit(solution)/shard_map/add | solution.py:21
  36.9 2.7 %copy-done = f32[128,3,4096]{0,2,1:T(8,128)} copy-done((f32[128,3,4096]{0,2,1:T(8,128)}, f32[128,3,4096]{0,2,1:T(8,128)S(1)}, u32[]{:S(2)}) %copy-start) | copy-done | bytes 6291480
  39.5 0.2 fusion.2
  39.7 0.5 copy.21
  40.3 16.9 %all_to_all.29 = bf16[128,4,1024]{2,0,1:T(8,128)(2,1)S(1)} all-to-all(bf16[128,4,1024]{2,0,1:T(8,128)(2,1)S(1)} %copy.21), channel_id=1, replica_groups=mesh['dp'=8,'ctx'=4] {'ctx'}, dimensions={1} | all-to-all | bytes 2097152 | tf_op jit(solution)/shard_map/all_to_all | solution.py:169
  57.2 0.8 copy.22
  58.0 0.3 reshape.46
  58.3 4.5 %fusion.8 = f32[1024,1024]{1,0:T(8,128)} fusion(bf16[1024,512]{1,0:T(8,128)(2,1)} %constant.9, bf16[512,1024]{1,0:T(8,128)(2,1)S(1)} %reshape.46), kind=kOutput, calls=%fused_computation.23 | convolution fusion | flops 1073741824 | bytes 6291456 | tf_op jit(solution)/shard_map/dot_general | solution.py:134
  62.8 2.9 %fusion.9 = f32[1024,1024]{1,0:T(8,128)S(1)} fusion(bf16[1024,512]{1,0:T(8,128)(2,1)} %constant.4.clone, bf16[512,1024]{1,0:T(8,128)(2,1)} %all-gather.2.cloned.1.call-done), kind=kOutput, calls=%fused_computation.24 | convolution fusion | flops 1073741824 | bytes 6291456 | tf_op jit(solution)/shard_map/dot_general | solution.py:135
  65.7 0.0 copy-done.1
  65.8 0.8 fusion.6
  66.6 0.2 copy-done.2
  66.8 0.9 fusion.4
  67.7 16.9 %all_to_all.30 = bf16[4,128,1024]{2,1,0:T(8,128)(2,1)S(1)} all-to-all(bf16[4,128,1024]{2,1,0:T(8,128)(2,1)S(1)} %bitcast.38), channel_id=1, replica_groups=mesh['dp'=8,'ctx'=4] {'ctx'}, dimensions={0} | all-to-all | bytes 2097152 | tf_op jit(solution)/shard_map/all_to_all | solution.py:171
  84.6 1.6 %convert_bitcast_fusion = f32[128,4,1024]{2,0,1:T(8,128)} fusion(bf16[4,128,1024]{2,1,0:T(8,128)(2,1)S(1)} %all_to_all.30), kind=kLoop, calls=%fused_computation.14 | loop fusion | flops 524288 | bytes 3145728 | tf_op jit(solution)/shard_map/convert_element_type | solution.py:156
  86.1 1.9 %copy.23 = f32[128,4,1024]{0,2,1:T(8,128)S(1)} copy(f32[128,4,1024]{2,0,1:T(8,128)} %convert_bitcast_fusion) | data formatting | bytes 4194304 | tf_op jit(solution)/shard_map/convert_element_type | solution.py:156
  88.1 2.0 %fusion.5 = bf16[1,128,4096]{1,2,0:T(8,128)(2,1)S(1)} fusion(f32[128,4,1024]{0,2,1:T(8,128)S(1)} %copy.23, f32[128,3,4096]{0,2,1:T(8,128)} %copy-done), kind=kLoop, calls=%fused_computation.13 | loop fusion | flops 1572864 | bytes 4194304 | tf_op jit(solution)/shard_map/convert_element_type | solution.py:156
  90.1 1.3 %copy.24 = bf16[1,128,4096]{2,1,0:T(8,128)(2,1)} copy(bf16[1,128,4096]{1,2,0:T(8,128)(2,1)S(1)} %fusion.5) | data formatting | bytes 2097152 | tf_op jit(solution)/shard_map/convert_element_type | solution.py:156
  (12 shorter events, 0.1 us)
Async XLA Ops:
  6.5 56.2 %all-gather.2.cloned.1.call-start = ((), (), s32[]{:S(2)}) async-start(), calls=%async_computation.2 | async-start | bytes 1179648 | tf_op jit(solution)/shard_map/all_gather | solution.py:163
  7.5 13.0 %collective-permute-start = (bf16[2,3,4096]{2,0,1:T(2,128)(2,1)S(1)}, bf16[2,3,4096]{2,0,1:T(2,128)(2,1)S(1)}, u32[]{:S(2)}, u32[]{:S(2)}) collective-permute-start(bf16[2,3,4096]{2,0,1:T(2,128)(2,1)S(1)} %slice_bitcast_fusion.3), channel_id=1, source_target_pairs={{0,1},{1,2},{2,3},{4,5},{5,6},{6,7},{8,9},{9,10},{10,11},{12,13},{... | collective-permute-start | bytes 147464 | tf_op jit(solution)/shard_map/ppermute | solution.py:165
  36.9 2.7 %copy-start = (f32[128,3,4096]{0,2,1:T(8,128)}, f32[128,3,4096]{0,2,1:T(8,128)S(1)}, u32[]{:S(2)}) copy-start(f32[128,3,4096]{0,2,1:T(8,128)S(1)} %fusion) | copy-start | bytes 18874372
  62.8 3.0 %copy-start.3 = (bf16[512,512]{1,0:T(8,128)(2,1)S(1)}, bf16[512,512]{1,0:T(8,128)(2,1)}, u32[]{:S(2)}) copy-start(bf16[512,512]{1,0:T(8,128)(2,1)} %constant.10) | copy-start | bytes 1572868
  62.8 3.0 %copy-start.1 = (f32[1024,1024]{1,0:T(8,128)S(1)}, f32[1024,1024]{1,0:T(8,128)}, u32[]{:S(2)}) copy-start(f32[1024,1024]{1,0:T(8,128)} %fusion.8) | copy-start | bytes 12582916
  65.8 1.0 %copy-start.2 = (bf16[512,512]{1,0:T(8,128)(2,1)S(1)}, bf16[512,512]{1,0:T(8,128)(2,1)}, u32[]{:S(2)}) copy-start(bf16[512,512]{1,0:T(8,128)(2,1)} %constant.11) | copy-start | bytes 1572868
  65.8 1.0 %copy-start.4 = (f32[1024]{0:T(1024)S(1)}, f32[1024]{0:T(1024)}, u32[]{:S(2)}) copy-start(f32[1024]{0:T(1024)} %param.9) | copy-start | bytes 12292
Sparse Core Ops, SparseCore 0:
  10.0 42.7 all-gather.1

commit v2 on v1

--- a/solution.py
+++ b/solution.py
@@ -1,9 +1,12 @@
+import functools
 import math
 
 import jax
 import jax.numpy as jnp
 import numpy as np
 from jax import lax
+from jax.experimental import pallas as pl
+from jax.experimental.pallas import tpu as pltpu
 from jax.sharding import PartitionSpec as P
 
 RADIX = 64
@@ -156,7 +159,7 @@
     return (query_part.astype(jnp.float32) * response_part.astype(jnp.float32)).astype(jnp.bfloat16)
 
 
-def on_device(projected, short_taps, long_filter, skip_gain):
+def on_device_large(projected, short_taps, long_filter, skip_gain):
     kernel_size = short_taps.shape[0]
     ctx_size = lax.axis_size("ctx")
     rows = projected[0]
@@ -172,6 +175,337 @@
     return combine_rows(queries, response)[None]
 
 
+CHUNK = 256
+MESH = pl.DeviceIdType.MESH
+
+
+def ctx_offsets(ctx_size):
+    pairs = [(a, b) for a in range(1, ctx_size // 2) for b in range(2)]
+    return pairs + [(0, 1)]
+
+
+def ctx_peer(me, offset, ctx_size, sign):
+    half = ctx_size // 2
+    chip = lax.rem(me // 2 + (half + sign * offset[0]) % half, half)
+    core = lax.rem(lax.rem(me, 2) + offset[1], 2)
+    return chip * 2 + core
+
+
+def mixer_kernel(
+    ctx_size,
+    dp_size,
+    x_hbm,
+    taps_ref,
+    filter_ref,
+    skip_ref,
+    forward_hbm,
+    backward_hbm,
+    out_ref,
+    x_ref,
+    forward_ref,
+    backward_ref,
+    taps_all,
+    halo_out,
+    halo_in,
+    gated_out,
+    gated_slab,
+    filter_slab,
+    filter_spec,
+    prod_ref,
+    response_slab,
+    response_in,
+    queries,
+    local_sem,
+    taps_send,
+    taps_recv,
+    halo_send,
+    halo_recv,
+    zfil_send,
+    zfil_recv,
+    yfil_send,
+    yfil_recv,
+    gated_send,
+    gated_recv,
+    resp_send,
+    resp_recv,
+):
+    kernel_size = taps_ref.shape[0]
+    channels = taps_ref.shape[2]
+    rows = x_ref.shape[1]
+    length = rows * ctx_size
+    chunks = channels // CHUNK
+    fil_rows = filter_ref.shape[0]
+    zsize = dp_size // 2
+    me = lax.axis_index("ctx")
+    dp = lax.axis_index("dp")
+    zpos, ypos = dp // 2, lax.rem(dp, 2)
+    offsets = ctx_offsets(ctx_size)
+    dests = [ctx_peer(me, o, ctx_size, 1) for o in offsets]
+    sources = [ctx_peer(me, o, ctx_size, -1) for o in offsets]
+    following = lax.rem(me + 1, ctx_size)
+    zpeers = [lax.rem(zpos + k, zsize) * 2 + ypos for k in range(1, zsize)]
+    zsources = [lax.rem(zpos + zsize - k, zsize) * 2 + ypos for k in range(1, zsize)]
+    ypeer = zpos * 2 + (1 - ypos)
+
+    x_copy = pltpu.make_async_copy(x_hbm, x_ref, local_sem.at[0])
+    x_copy.start()
+    forward_copy = pltpu.make_async_copy(forward_hbm, forward_ref, local_sem.at[1])
+    forward_copy.start()
+    backward_copy = pltpu.make_async_copy(backward_hbm, backward_ref, local_sem.at[2])
+    backward_copy.start()
+
+    barrier = pltpu.get_barrier_semaphore()
+    for dest in dests:
+        pl.semaphore_signal(barrier, inc=1, device_id={"ctx": dest}, device_id_type=MESH)
+    for peer in zpeers + [ypeer]:
+        pl.semaphore_signal(barrier, inc=1, device_id={"dp": peer}, device_id_type=MESH)
+    pl.semaphore_wait(barrier, len(dests) + len(zpeers) + 1)
+
+    def taps_copy(i, slot):
+        return pltpu.make_async_remote_copy(
+            src_ref=taps_ref,
+            dst_ref=taps_all.at[slot],
+            send_sem=taps_send.at[i],
+            recv_sem=taps_recv.at[i],
+            device_id={"ctx": dests[i]},
+            device_id_type=MESH,
+        )
+
+    def filter_block(block):
+        return filter_slab.at[pl.ds(pl.multiple_of(block * fil_rows, fil_rows), fil_rows), :]
+
+    def zfil_copy(k, block):
+        return pltpu.make_async_remote_copy(
+            src_ref=filter_ref,
+            dst_ref=filter_block(block),
+            send_sem=zfil_send.at[k],
+            recv_sem=zfil_recv.at[k],
+            device_id={"dp": zpeers[k]},
+            device_id_type=MESH,
+        )
+
+    def yfil_copy(k, source, block):
+        return pltpu.make_async_remote_copy(
+            src_ref=source,
+            dst_ref=filter_block(block),
+            send_sem=yfil_send.at[k],
+            recv_sem=yfil_recv.at[k],
+            device_id={"dp": ypeer},
+            device_id_type=MESH,
+        )
+
+    for i in range(len(offsets)):
+        taps_copy(i, me).start()
+    x_copy.wait()
+    halo_out[...] = x_ref[:, rows - (kernel_size - 1) :, :]
+    halo_copy = pltpu.make_async_remote_copy(
+        src_ref=halo_out,
+        dst_ref=halo_in,
+        send_sem=halo_send,
+        recv_sem=halo_recv,
+        device_id={"ctx": following},
+        device_id_type=MESH,
+    )
+    halo_copy.start()
+    for k in range(zsize - 1):
+        zfil_copy(k, dp).start()
+    yfil_copy(0, filter_ref, dp).start()
+    taps_all[me] = taps_ref[...]
+    filter_block(dp)[...] = filter_ref[...]
+    for i in range(len(offsets)):
+        taps_copy(i, sources[i]).wait_recv()
+    halo_copy.wait_recv()
+
+    row_index = lax.broadcasted_iota(jnp.int32, (rows, CHUNK), 0)
+
+    def short_filter(stream, owner, chunk):
+        columns = pl.ds(pl.multiple_of(owner * channels + chunk * CHUNK, CHUNK), CHUNK)
+        taps_columns = pl.ds(pl.multiple_of(chunk * CHUNK, CHUNK), CHUNK)
+        values = x_ref[stream, :, columns].astype(jnp.float32)
+        edge = halo_in[stream, :, columns].astype(jnp.float32)
+        edge = jnp.where(me > 0, edge, jnp.zeros_like(edge))
+        total = taps_all[owner, 0, stream : stream + 1, taps_columns] * values
+        for tap in range(1, kernel_size):
+            moved = pltpu.roll(values, tap, 0)
+            for row in range(tap):
+                at = kernel_size - 1 + row - tap
+                moved = jnp.where(row_index == row, edge[at : at + 1], moved)
+            total = total + taps_all[owner, tap, stream : stream + 1, taps_columns] * moved
+        return total
+
+    def gated_rows(owner, chunk):
+        return (short_filter(1, owner, chunk) * short_filter(2, owner, chunk)).astype(jnp.bfloat16)
+
+    def position_rows(owner):
+        return pl.ds(pl.multiple_of(owner * rows, rows), rows)
+
+    def gated_copy(i, chunk, owner):
+        return pltpu.make_async_remote_copy(
+            src_ref=gated_out.at[i, chunk],
+            dst_ref=gated_slab.at[chunk, position_rows(owner), :],
+            send_sem=gated_send.at[i, chunk],
+            recv_sem=gated_recv.at[i, chunk],
+            device_id={"ctx": dests[i]},
+            device_id_type=MESH,
+        )
+
+    def response_copy(i, chunk):
+        return pltpu.make_async_remote_copy(
+            src_ref=response_slab.at[chunk, position_rows(dests[i]), :],
+            dst_ref=response_in.at[i, chunk],
+            send_sem=resp_send.at[i, chunk],
+            recv_sem=resp_recv.at[i, chunk],
+            device_id={"ctx": dests[i]},
+            device_id_type=MESH,
+        )
+
+    def push_gated(chunk, carry):
+        for i in range(len(offsets)):
+            gated_out[i, chunk] = gated_rows(dests[i], chunk)
+            gated_copy(i, chunk, me).start()
+        gated_slab[chunk, position_rows(me), :] = gated_rows(me, chunk)
+        return carry
+
+    lax.fori_loop(0, chunks, push_gated, 0)
+
+    def make_queries(step, carry):
+        owner, chunk = step // chunks, lax.rem(step, chunks)
+        queries[owner, chunk] = short_filter(0, owner, chunk).astype(jnp.bfloat16)
+        return carry
+
+    for k in range(zsize - 1):
+        zfil_copy(k, zsources[k]).wait_recv()
+        yfil_copy(k + 1, filter_block(zsources[k]), zsources[k]).start()
+    lax.fori_loop(0, chunks * ctx_size, make_queries, 0)
+    forward_copy.wait()
+    yfil_copy(0, filter_ref, ypeer).wait_recv()
+    for k in range(zsize - 1):
+        block = zsources[k] - ypos + (1 - ypos)
+        yfil_copy(k + 1, filter_ref, block).wait_recv()
+
+    def filter_spectrum(chunk, carry):
+        columns = pl.ds(pl.multiple_of(chunk * CHUNK, CHUNK), CHUNK)
+        filter_spec[chunk] = jnp.dot(
+            forward_ref[...], filter_slab[:, columns], preferred_element_type=jnp.float32
+        )
+        return carry
+
+    lax.fori_loop(0, chunks, filter_spectrum, 0)
+    backward_copy.wait()
+
+    def convolve(chunk, carry):
+        for i in range(len(offsets)):
+            gated_copy(i, chunk, sources[i]).wait_recv()
+        gated = gated_slab[chunk]
+        sig_cos = jnp.dot(forward_ref[:length], gated, preferred_element_type=jnp.float32)
+        sig_sin = jnp.dot(forward_ref[length:], gated, preferred_element_type=jnp.float32)
+        ker_cos, ker_sin = filter_spec[chunk, :length], filter_spec[chunk, length:]
+        prod_ref[:length] = (sig_cos * ker_cos - sig_sin * ker_sin).astype(jnp.bfloat16)
+        prod_ref[length:] = (sig_cos * ker_sin + sig_sin * ker_cos).astype(jnp.bfloat16)
+        long_part = jnp.dot(backward_ref[...], prod_ref[...], preferred_element_type=jnp.float32)
+        columns = pl.ds(pl.multiple_of(chunk * CHUNK, CHUNK), CHUNK)
+        direct = skip_ref[:, columns] * gated.astype(jnp.float32)
+        response_slab[chunk] = (long_part + direct).astype(jnp.bfloat16)
+        for i in range(len(offsets)):
+            response_copy(i, chunk).start()
+        mix_into(me, chunk, response_slab[chunk, position_rows(me), :])
+        return carry
+
+    def mix_into(owner, chunk, response):
+        columns = pl.ds(pl.multiple_of(owner * channels + chunk * CHUNK, CHUNK), CHUNK)
+        mixed = queries[owner, chunk].astype(jnp.float32) * response.astype(jnp.float32)
+        out_ref[:, columns] = mixed.astype(jnp.bfloat16)
+
+    lax.fori_loop(0, chunks, convolve, 0)
+
+    def finish(chunk, carry):
+        for i in reversed(range(len(offsets))):
+            response_copy(i, chunk).wait_recv()
+            mix_into(sources[i], chunk, response_in[i, chunk])
+        return carry
+
+    lax.fori_loop(0, chunks, finish, 0)
+
+    def drain(chunk, carry):
+        for i in range(len(offsets)):
+            gated_copy(i, chunk, me).wait_send()
+            response_copy(i, chunk).wait_send()
+        return carry
+
+    lax.fori_loop(0, chunks, drain, 0)
+    for i in range(len(offsets)):
+        taps_copy(i, me).wait_send()
+    halo_copy.wait_send()
+    for k in range(zsize - 1):
+        zfil_copy(k, dp).wait_send()
+    yfil_copy(0, filter_ref, dp).wait_send()
+    for k in range(zsize - 1):
+        yfil_copy(k + 1, filter_block(zsources[k]), zsources[k]).wait_send()
+
+
+def on_device(projected, short_taps, long_filter, skip_gain):
+    ctx_size, dp_size = lax.axis_size("ctx"), lax.axis_size("dp")
+    kernel_size, streams, channels = short_taps.shape
+    rows, width = projected.shape[1], projected.shape[3]
+    length = rows * ctx_size
+    regular = ctx_size % 2 == 0 and dp_size % 2 == 0 and channels % CHUNK == 0
+    if length > 1024 or not regular:
+        return on_device_large(projected, short_taps, long_filter, skip_gain)
+    forward, backward = quarter_tables(length)
+    chunks = channels // CHUNK
+    peers = ctx_size - 1
+    zsize = dp_size // 2
+    any_spec = pl.BlockSpec(memory_space=pl.ANY)
+    vmem_spec = pl.BlockSpec(memory_space=pltpu.VMEM)
+    dma = pltpu.SemaphoreType.DMA
+    mixed = pl.pallas_call(
+        functools.partial(mixer_kernel, ctx_size, dp_size),
+        out_shape=jax.ShapeDtypeStruct((rows, width), jnp.bfloat16),
+        in_specs=[any_spec, vmem_spec, vmem_spec, vmem_spec, any_spec, any_spec],
+        out_specs=vmem_spec,
+        scratch_shapes=[
+            pltpu.VMEM((streams, rows, width), jnp.bfloat16),
+            pltpu.VMEM(forward.shape, jnp.bfloat16),
+            pltpu.VMEM(backward.shape, jnp.bfloat16),
+            pltpu.VMEM((ctx_size, kernel_size, streams, channels), jnp.float32),
+            pltpu.VMEM((streams, kernel_size - 1, width), jnp.bfloat16),
+            pltpu.VMEM((streams, kernel_size - 1, width), jnp.bfloat16),
+            pltpu.VMEM((peers, chunks, rows, CHUNK), jnp.bfloat16),
+            pltpu.VMEM((chunks, length, CHUNK), jnp.bfloat16),
+            pltpu.VMEM((length, channels), jnp.bfloat16),
+            pltpu.VMEM((chunks, 2 * length, CHUNK), jnp.float32),
+            pltpu.VMEM((2 * length, CHUNK), jnp.bfloat16),
+            pltpu.VMEM((chunks, length, CHUNK), jnp.bfloat16),
+            pltpu.VMEM((peers, chunks, rows, CHUNK), jnp.bfloat16),
+            pltpu.VMEM((ctx_size, chunks, rows, CHUNK), jnp.bfloat16),
+            dma((3,)),
+            dma((peers,)),
+            dma((peers,)),
+            dma,
+            dma,
+            dma((zsize - 1,)),
+            dma((zsize - 1,)),
+            dma((zsize,)),
+            dma((zsize,)),
+            dma((peers, chunks)),
+            dma((peers, chunks)),
+            dma((peers, chunks)),
+            dma((peers, chunks)),
+        ],
+        compiler_params=pltpu.CompilerParams(
+            collective_id=0, has_side_effects=True, vmem_limit_bytes=48 * 2**20
+        ),
+    )(
+        projected[0].transpose(1, 0, 2),
+        short_taps,
+        long_filter,
+        skip_gain[None],
+        forward,
+        backward,
+    )
+    return mixed[None]
+
+
 def solution(mesh):
     return jax.shard_map(
         on_device,

time: 98.7 us -> 43.5 us (0.44)
  blocking collectives: 40.9 us -> 0 us
  Pallas kernels: 0 us -> 36.9 us
  other arithmetic: 17.3 us -> 0 us
  between operations: 13.5 us -> 0.01 us
  local copies, waits for them, and re-layouts: 15.1 us -> 5.81 us
  matrix products: 9.08 us -> 0 us
  starting transfers between devices: 2.36 us -> 0 us
    pallas_call x0 -> x1, Pallas kernels: none -> 36.9 us  [on_device(): pl.pallas_call(functools.partial(mixer_kernel, ctx_size, dp_size), out_sh...]
    all_to_all x2 -> x0, blocking collectives: 33.8 us -> none  [the longest x1 16.9 us: on_device(): lax.all_to_all(response_slab, 'ctx', split_axis=0, concat_axis=1, tiled=T...]
    add x1 -> x0, other arithmetic: 9.39 us -> none  [causal_short(): summed = summed + taps[tap_index] * widened[offset:offset + row_count]]
    dot_general x4 -> x0, matrix products: 9.08 us -> none  [the longest x1 4.5 us: long_convolve(): sig = jnp.dot(forward, gated_slab, preferred_element_type=jnp.float32)]
    convert_element_type x4 -> x0, other arithmetic: 7.92 us -> none  [the longest x1 4.08 us: causal_short(): widened = extended.astype(jnp.float32)]
    all_gather x1 -> x0, blocking collectives: 7.11 us -> none  [on_device(): all_taps = lax.all_gather(short_taps, 'ctx', axis=2, tiled=True)]
    convert_element_type x3 -> x0, local copies, waits for them, and re-layouts: 3.75 us -> none  [the longest x1 1.91 us: combine_rows(): response_part.astype(jnp.float32)]
    ppermute x1 -> x0, local copies, waits for them, and re-layouts: 2.8 us -> none  [on_device(): lax.ppermute(rows[-(kernel_size - 1):], 'ctx', [(i, i + 1) for i in range...]
  transfers between devices with their start and end apart: 2 -> 0, of which waited for: 0 -> 0; matrix products, arithmetic and copies ran while one was open for 27% -> 0% of each run, Pallas kernels for 0% -> 0%
where the time goes in v2:
time: 43.5 us; the launch traced here: 42.7 us
  Pallas kernels  36.9 us (85%)
  local copies, waits for them, and re-layouts  5.81 us (13%)
    pallas_call x1, Pallas kernels, on_device(): pl.pallas_call(functools.partial(mixer_kernel, ctx_size, dp_size), out_sh...  36.9 us
    unnamed x11, local copies, waits for them, and re-layouts  5.81 us

profile of v2, /device:TPU:0, one launch (start us, length us, event | category | flops | bytes accessed | tf_op | source)
XLA Modules:
  0.0 42.7 jit_solution(8832754932002651583)
XLA Ops:
  0.0 0.0 copy-start
  0.0 1.2 %copy-done = bf16[512,1024]{1,0:T(8,128)(2,1)S(1)} copy-done((bf16[512,1024]{1,0:T(8,128)(2,1)S(1)}, bf16[512,1024]{1,0:T(8,128)(2,1)}, u32[]{:S(2)}) %copy-start) | copy-done | bytes 1048600
  1.2 0.0 copy-start.1
  1.2 1.2 %copy-done.1 = bf16[1024,512]{1,0:T(8,128)(2,1)S(1)} copy-done((bf16[1024,512]{1,0:T(8,128)(2,1)S(1)}, bf16[1024,512]{1,0:T(8,128)(2,1)}, u32[]{:S(2)}) %copy-start.1) | copy-done | bytes 1048600
  2.5 0.0 copy-start.2
  2.5 0.9 %copy-done.2 = bf16[64,1024]{1,0:T(8,128)(2,1)S(1)} copy-done((bf16[64,1024]{1,0:T(8,128)(2,1)S(1)}, bf16[64,1024]{1,0:T(8,128)(2,1)}, u32[]{:S(2)}) %copy-start.2) | copy-done | bytes 131096
  3.4 0.0 copy-start.3
  3.4 0.8 %copy-done.3 = f32[3,3,1024]{2,1,0:T(4,128)S(1)} copy-done((f32[3,3,1024]{2,1,0:T(4,128)S(1)}, f32[3,3,1024]{2,1,0:T(4,128)}, u32[]{:S(2)}) %copy-start.3) | copy-done | bytes 36888
  4.2 0.0 copy-start.4
  4.2 0.7 %copy-done.4 = f32[1024]{0:T(1024)S(1)} copy-done((f32[1024]{0:T(1024)S(1)}, f32[1024]{0:T(1024)}, u32[]{:S(2)}) %copy-start.4) | copy-done | bytes 4120
  4.8 36.9 %shard_map.64 = bf16[128,4096]{1,0:T(8,128)(2,1)S(1)} custom-call(bf16[3,128,4096]{2,1,0:T(8,128)(2,1)} %bitcast.7, f32[3,3,1024]{2,1,0:T(4,128)S(1)} %copy-done.3, bf16[64,1024]{1,0:T(8,128)(2,1)S(1)} %copy-done.2, f32[1,1024]{1,0:T(1,128)S(1)} %bitcast.6, bf16[1024,512]{1,0:T(8,128)(2,1)S(1)} %copy-done.1, bf16[512,1024]{1,0:T(8,128)(2,1)S(1)} %copy-done), custom_call_target="tpu_custom_call" | custom-call | tf_op jit(solution)/shard_map/pallas_call | solution.py:461
  41.7 1.0 %copy.8 = bf16[1,128,4096]{2,1,0:T(8,128)(2,1)} copy(bf16[1,128,4096]{2,1,0:T(8,128)(2,1)S(1)} %bitcast.5) | data formatting | bytes 2097152
Async XLA Ops:
  0.0 1.2 %copy-start = (bf16[512,1024]{1,0:T(8,128)(2,1)S(1)}, bf16[512,1024]{1,0:T(8,128)(2,1)}, u32[]{:S(2)}) copy-start(bf16[512,1024]{1,0:T(8,128)(2,1)} %constant.5.clone.backward_hbm) | copy-start | bytes 3145732
  1.2 1.2 %copy-start.1 = (bf16[1024,512]{1,0:T(8,128)(2,1)S(1)}, bf16[1024,512]{1,0:T(8,128)(2,1)}, u32[]{:S(2)}) copy-start(bf16[1024,512]{1,0:T(8,128)(2,1)} %constant.4.clone.forward_hbm) | copy-start | bytes 3145732
  2.5 0.9 %copy-start.2 = (bf16[64,1024]{1,0:T(8,128)(2,1)S(1)}, bf16[64,1024]{1,0:T(8,128)(2,1)}, u32[]{:S(2)}) copy-start(bf16[64,1024]{1,0:T(8,128)(2,1)} %filter_ref.1) | copy-start | bytes 393220
  3.4 0.8 %copy-start.3 = (f32[3,3,1024]{2,1,0:T(4,128)S(1)}, f32[3,3,1024]{2,1,0:T(4,128)}, u32[]{:S(2)}) copy-start(f32[3,3,1024]{2,1,0:T(4,128)} %taps_ref.1) | copy-start | bytes 110596
  4.2 0.7 %copy-start.4 = (f32[1024]{0:T(1024)S(1)}, f32[1024]{0:T(1024)}, u32[]{:S(2)}) copy-start(f32[1024]{0:T(1024)} %param.9) | copy-start | bytes 12292

commit v3 on v2

--- a/solution.py
+++ b/solution.py
@@ -197,11 +197,12 @@
     x_hbm,
     taps_ref,
     filter_ref,
-    skip_ref,
+    skip_hbm,
     forward_hbm,
     backward_hbm,
-    out_ref,
+    out_hbm,
     x_ref,
+    skip_ref,
     forward_ref,
     backward_ref,
     taps_all,
@@ -228,6 +229,8 @@
     gated_recv,
     resp_send,
     resp_recv,
+    out_sem,
+    filter_sem,
 ):
     kernel_size = taps_ref.shape[0]
     channels = taps_ref.shape[2]
@@ -243,9 +246,20 @@
     dests = [ctx_peer(me, o, ctx_size, 1) for o in offsets]
     sources = [ctx_peer(me, o, ctx_size, -1) for o in offsets]
     following = lax.rem(me + 1, ctx_size)
-    zpeers = [lax.rem(zpos + k, zsize) * 2 + ypos for k in range(1, zsize)]
-    zsources = [lax.rem(zpos + zsize - k, zsize) * 2 + ypos for k in range(1, zsize)]
     ypeer = zpos * 2 + (1 - ypos)
+
+    def filter_block(block, chunk):
+        return filter_slab.at[
+            chunk, pl.ds(pl.multiple_of(block * fil_rows, fil_rows), fil_rows), :
+        ]
+
+    def own_filter(chunk):
+        return filter_ref.at[:, pl.ds(pl.multiple_of(chunk * CHUNK, CHUNK), CHUNK)]
+
+    def own_filter_copy(chunk):
+        return pltpu.make_async_copy(
+            own_filter(chunk), filter_block(dp, chunk), filter_sem.at[chunk]
+        )
 
     x_copy = pltpu.make_async_copy(x_hbm, x_ref, local_sem.at[0])
     x_copy.start()
@@ -253,49 +267,87 @@
     forward_copy.start()
     backward_copy = pltpu.make_async_copy(backward_hbm, backward_ref, local_sem.at[2])
     backward_copy.start()
+    skip_copy = pltpu.make_async_copy(skip_hbm, skip_ref, local_sem.at[3])
+    skip_copy.start()
+    own_taps_copy = pltpu.make_async_copy(taps_ref, taps_all.at[me], local_sem.at[4])
+    own_taps_copy.start()
+    for chunk in range(chunks):
+        own_filter_copy(chunk).start()
 
     barrier = pltpu.get_barrier_semaphore()
     for dest in dests:
         pl.semaphore_signal(barrier, inc=1, device_id={"ctx": dest}, device_id_type=MESH)
-    for peer in zpeers + [ypeer]:
-        pl.semaphore_signal(barrier, inc=1, device_id={"dp": peer}, device_id_type=MESH)
-    pl.semaphore_wait(barrier, len(dests) + len(zpeers) + 1)
-
-    def taps_copy(i, slot):
+    pl.semaphore_signal(barrier, inc=1, device_id={"dp": ypeer}, device_id_type=MESH)
+
+    for turn in (1, zsize - 1):
+        side_peer = lax.rem(zpos + turn, zsize) * 2 + ypos
+        pl.semaphore_signal(barrier, inc=1, device_id={"dp": side_peer}, device_id_type=MESH)
+    pl.semaphore_wait(barrier, len(dests) + 3)
+
+    def taps_copy(i, source, slot):
         return pltpu.make_async_remote_copy(
-            src_ref=taps_ref,
+            src_ref=source,
             dst_ref=taps_all.at[slot],
             send_sem=taps_send.at[i],
             recv_sem=taps_recv.at[i],
-            device_id={"ctx": dests[i]},
+            device_id={"ctx": dests[i] if offsets[i][1] == 0 else dests[-1]},
             device_id_type=MESH,
         )
 
-    def filter_block(block):
-        return filter_slab.at[pl.ds(pl.multiple_of(block * fil_rows, fil_rows), fil_rows), :]
-
-    def zfil_copy(k, block):
-        return pltpu.make_async_remote_copy(
-            src_ref=filter_ref,
-            dst_ref=filter_block(block),
-            send_sem=zfil_send.at[k],
-            recv_sem=zfil_recv.at[k],
-            device_id={"dp": zpeers[k]},
-            device_id_type=MESH,
-        )
-
-    def yfil_copy(k, source, block):
+    def zfil_copy(side, step, source, block, chunk):
         return pltpu.make_async_remote_copy(
             src_ref=source,
-            dst_ref=filter_block(block),
-            send_sem=yfil_send.at[k],
-            recv_sem=yfil_recv.at[k],
+            dst_ref=filter_block(block, chunk),
+            send_sem=zfil_send.at[side, step, chunk],
+            recv_sem=zfil_recv.at[side, step, chunk],
+            device_id={"dp": dp + 2 - 4 * side},
+            device_id_type=MESH,
+        )
+
+    def yfil_copy(side, step, source, block, chunk):
+        return pltpu.make_async_remote_copy(
+            src_ref=source,
+            dst_ref=filter_block(block, chunk),
+            send_sem=yfil_send.at[side, step, chunk],
+            recv_sem=yfil_recv.at[side, step, chunk],
             device_id={"dp": ypeer},
             device_id_type=MESH,
         )
 
-    for i in range(len(offsets)):
-        taps_copy(i, me).start()
+    has_next = (zpos < zsize - 1, zpos > 0)
+
+    def origin(side, step):
+        return zpos - step if side == 0 else zpos + step
+
+    def present(side, step):
+        return zpos >= step if side == 0 else zpos + step < zsize
+
+    def forward_filter(step, chunk):
+        for side in range(2):
+
+            @pl.when(present(side, step))
+            def _(side=side):
+                block = origin(side, step) * 2 + ypos
+                source = filter_block(block, chunk)
+                zfil_copy(side, step - 1, own_filter(chunk), block, chunk).wait_recv()
+                yfil_copy(side, step, source, block, chunk).start()
+
+                @pl.when(has_next[side])
+                def _():
+                    zfil_copy(side, step, source, block, chunk).start()
+
+    direct = [i for i, offset in enumerate(offsets) if offset[1] == 0 or offset[0] == 0]
+    relayed = [i for i in range(len(offsets)) if i not in direct]
+    for i in direct:
+        taps_copy(i, taps_ref, me).start()
+    for chunk in range(chunks):
+        yfil_copy(0, 0, own_filter(chunk), dp, chunk).start()
+        for side in range(2):
+
+            @pl.when(has_next[side])
+            def _(side=side, chunk=chunk):
+                zfil_copy(side, 0, own_filter(chunk), dp, chunk).start()
+
     x_copy.wait()
     halo_out[...] = x_ref[:, rows - (kernel_size - 1) :, :]
     halo_copy = pltpu.make_async_remote_copy(
@@ -307,13 +359,11 @@
         device_id_type=MESH,
     )
     halo_copy.start()
-    for k in range(zsize - 1):
-        zfil_copy(k, dp).start()
-    yfil_copy(0, filter_ref, dp).start()
-    taps_all[me] = taps_ref[...]
-    filter_block(dp)[...] = filter_ref[...]
-    for i in range(len(offsets)):
-        taps_copy(i, sources[i]).wait_recv()
+    own_taps_copy.wait()
+    for i in direct:
+        taps_copy(i, taps_ref, sources[i]).wait_recv()
+    for i in relayed:
+        taps_copy(i, taps_all.at[sources[i - 1]], sources[i - 1]).start()
     halo_copy.wait_recv()
 
     row_index = lax.broadcasted_iota(jnp.int32, (rows, CHUNK), 0)
@@ -359,51 +409,68 @@
             device_id_type=MESH,
         )
 
-    def push_gated(chunk, carry):
+    def push_gated(i, chunk):
+        gated_out[i, chunk] = gated_rows(dests[i], chunk)
+        gated_copy(i, chunk, me).start()
+
+    for i in direct:
+        push_gated(i, 0)
+    for i in relayed:
+        taps_copy(i, taps_ref, sources[i]).wait_recv()
+        push_gated(i, 0)
+    gated_slab[0, position_rows(me), :] = gated_rows(me, 0)
+
+    forward_filter(1, 0)
+
+    def push_chunk(chunk, carry):
         for i in range(len(offsets)):
-            gated_out[i, chunk] = gated_rows(dests[i], chunk)
-            gated_copy(i, chunk, me).start()
+            push_gated(i, chunk)
+        forward_filter(1, chunk)
         gated_slab[chunk, position_rows(me), :] = gated_rows(me, chunk)
         return carry
 
-    lax.fori_loop(0, chunks, push_gated, 0)
-
-    def make_queries(step, carry):
-        owner, chunk = step // chunks, lax.rem(step, chunks)
-        queries[owner, chunk] = short_filter(0, owner, chunk).astype(jnp.bfloat16)
-        return carry
-
-    for k in range(zsize - 1):
-        zfil_copy(k, zsources[k]).wait_recv()
-        yfil_copy(k + 1, filter_block(zsources[k]), zsources[k]).start()
-    lax.fori_loop(0, chunks * ctx_size, make_queries, 0)
+    lax.fori_loop(1, chunks, push_chunk, 0)
+
+    def fill_queries(chunk, carry):
+        forward_filter(2, chunk)
+
+        def one_owner(owner, inner):
+            queries[owner, chunk] = short_filter(0, owner, chunk).astype(jnp.bfloat16)
+            return inner
+
+        return lax.fori_loop(0, ctx_size, one_owner, carry)
+
+    lax.fori_loop(0, chunks, fill_queries, 0)
+    for step in range(3, zsize):
+        lax.fori_loop(0, chunks, lambda chunk, _: forward_filter(step, chunk) or 0, 0)
     forward_copy.wait()
-    yfil_copy(0, filter_ref, ypeer).wait_recv()
-    for k in range(zsize - 1):
-        block = zsources[k] - ypos + (1 - ypos)
-        yfil_copy(k + 1, filter_ref, block).wait_recv()
-
-    def filter_spectrum(chunk, carry):
+    backward_copy.wait()
+    skip_copy.wait()
+
+    def convolve(chunk, carry):
         columns = pl.ds(pl.multiple_of(chunk * CHUNK, CHUNK), CHUNK)
-        filter_spec[chunk] = jnp.dot(
-            forward_ref[...], filter_slab[:, columns], preferred_element_type=jnp.float32
-        )
-        return carry
-
-    lax.fori_loop(0, chunks, filter_spectrum, 0)
-    backward_copy.wait()
-
-    def convolve(chunk, carry):
+        own_filter_copy(chunk).wait()
+        yfil_copy(0, 0, own_filter(chunk), ypeer, chunk).wait_recv()
+        for side in range(2):
+            for step in range(1, zsize):
+
+                @pl.when(present(side, step))
+                def _(side=side, step=step):
+                    block = origin(side, step) * 2 + 1 - ypos
+                    yfil_copy(side, step, own_filter(chunk), block, chunk).wait_recv()
+
+        filter_spec[...] = jnp.dot(
+            forward_ref[...], filter_slab[chunk], preferred_element_type=jnp.float32
+        )
         for i in range(len(offsets)):
             gated_copy(i, chunk, sources[i]).wait_recv()
         gated = gated_slab[chunk]
         sig_cos = jnp.dot(forward_ref[:length], gated, preferred_element_type=jnp.float32)
         sig_sin = jnp.dot(forward_ref[length:], gated, preferred_element_type=jnp.float32)
-        ker_cos, ker_sin = filter_spec[chunk, :length], filter_spec[chunk, length:]
+        ker_cos, ker_sin = filter_spec[:length], filter_spec[length:]
         prod_ref[:length] = (sig_cos * ker_cos - sig_sin * ker_sin).astype(jnp.bfloat16)
         prod_ref[length:] = (sig_cos * ker_sin + sig_sin * ker_cos).astype(jnp.bfloat16)
         long_part = jnp.dot(backward_ref[...], prod_ref[...], preferred_element_type=jnp.float32)
-        columns = pl.ds(pl.multiple_of(chunk * CHUNK, CHUNK), CHUNK)
         direct = skip_ref[:, columns] * gated.astype(jnp.float32)
         response_slab[chunk] = (long_part + direct).astype(jnp.bfloat16)
         for i in range(len(offsets)):
@@ -411,10 +478,16 @@
         mix_into(me, chunk, response_slab[chunk, position_rows(me), :])
         return carry
 
+    def out_copy(owner, chunk):
+        columns = pl.ds(pl.multiple_of(owner * channels + chunk * CHUNK, CHUNK), CHUNK)
+        return pltpu.make_async_copy(
+            queries.at[owner, chunk], out_hbm.at[:, columns], out_sem.at[owner, chunk]
+        )
+
     def mix_into(owner, chunk, response):
-        columns = pl.ds(pl.multiple_of(owner * channels + chunk * CHUNK, CHUNK), CHUNK)
         mixed = queries[owner, chunk].astype(jnp.float32) * response.astype(jnp.float32)
-        out_ref[:, columns] = mixed.astype(jnp.bfloat16)
+        queries[owner, chunk] = mixed.astype(jnp.bfloat16)
+        out_copy(owner, chunk).start()
 
     lax.fori_loop(0, chunks, convolve, 0)
 
@@ -430,17 +503,33 @@
         for i in range(len(offsets)):
             gated_copy(i, chunk, me).wait_send()
             response_copy(i, chunk).wait_send()
+        for owner in range(ctx_size):
+            out_copy(owner, chunk).wait()
+        yfil_copy(0, 0, own_filter(chunk), dp, chunk).wait_send()
+        for side in range(2):
+
+            @pl.when(has_next[side])
+            def _(side=side):
+                zfil_copy(side, 0, own_filter(chunk), dp, chunk).wait_send()
+
+            for step in range(1, zsize):
+
+                @pl.when(present(side, step))
+                def _(side=side, step=step):
+                    block = origin(side, step) * 2 + ypos
+                    source = filter_block(block, chunk)
+                    yfil_copy(side, step, source, block, chunk).wait_send()
+
+                    @pl.when(has_next[side])
+                    def _():
+                        zfil_copy(side, step, source, block, chunk).wait_send()
+
         return carry
 
     lax.fori_loop(0, chunks, drain, 0)
     for i in range(len(offsets)):
-        taps_copy(i, me).wait_send()
+        taps_copy(i, taps_ref, me).wait_send()
     halo_copy.wait_send()
-    for k in range(zsize - 1):
-        zfil_copy(k, dp).wait_send()
-    yfil_copy(0, filter_ref, dp).wait_send()
-    for k in range(zsize - 1):
-        yfil_copy(k + 1, filter_block(zsources[k]), zsources[k]).wait_send()
 
 
 def on_device(projected, short_taps, long_filter, skip_gain):
@@ -448,23 +537,23 @@
     kernel_size, streams, channels = short_taps.shape
     rows, width = projected.shape[1], projected.shape[3]
     length = rows * ctx_size
-    regular = ctx_size % 2 == 0 and dp_size % 2 == 0 and channels % CHUNK == 0
+    regular = ctx_size % 2 == 0 and dp_size % 2 == 0 and dp_size >= 6 and channels % CHUNK == 0
     if length > 1024 or not regular:
         return on_device_large(projected, short_taps, long_filter, skip_gain)
     forward, backward = quarter_tables(length)
     chunks = channels // CHUNK
     peers = ctx_size - 1
     zsize = dp_size // 2
-    any_spec = pl.BlockSpec(memory_space=pl.ANY)
-    vmem_spec = pl.BlockSpec(memory_space=pltpu.VMEM)
+    hbm_spec = pl.BlockSpec(memory_space=pltpu.HBM)
     dma = pltpu.SemaphoreType.DMA
     mixed = pl.pallas_call(
         functools.partial(mixer_kernel, ctx_size, dp_size),
         out_shape=jax.ShapeDtypeStruct((rows, width), jnp.bfloat16),
-        in_specs=[any_spec, vmem_spec, vmem_spec, vmem_spec, any_spec, any_spec],
-        out_specs=vmem_spec,
+        in_specs=[hbm_spec] * 6,
+        out_specs=hbm_spec,
         scratch_shapes=[
             pltpu.VMEM((streams, rows, width), jnp.bfloat16),
+            pltpu.VMEM((1, channels), jnp.float32),
             pltpu.VMEM(forward.shape, jnp.bfloat16),
             pltpu.VMEM(backward.shape, jnp.bfloat16),
             pltpu.VMEM((ctx_size, kernel_size, streams, channels), jnp.float32),
@@ -472,28 +561,30 @@
             pltpu.VMEM((streams, kernel_size - 1, width), jnp.bfloat16),
             pltpu.VMEM((peers, chunks, rows, CHUNK), jnp.bfloat16),
             pltpu.VMEM((chunks, length, CHUNK), jnp.bfloat16),
-            pltpu.VMEM((length, channels), jnp.bfloat16),
-            pltpu.VMEM((chunks, 2 * length, CHUNK), jnp.float32),
+            pltpu.VMEM((chunks, length, CHUNK), jnp.bfloat16),
+            pltpu.VMEM((2 * length, CHUNK), jnp.float32),
             pltpu.VMEM((2 * length, CHUNK), jnp.bfloat16),
             pltpu.VMEM((chunks, length, CHUNK), jnp.bfloat16),
             pltpu.VMEM((peers, chunks, rows, CHUNK), jnp.bfloat16),
             pltpu.VMEM((ctx_size, chunks, rows, CHUNK), jnp.bfloat16),
-            dma((3,)),
+            dma((5,)),
             dma((peers,)),
             dma((peers,)),
             dma,
             dma,
-            dma((zsize - 1,)),
-            dma((zsize - 1,)),
-            dma((zsize,)),
-            dma((zsize,)),
+            dma((2, zsize, chunks)),
+            dma((2, zsize, chunks)),
+            dma((2, zsize, chunks)),
+            dma((2, zsize, chunks)),
             dma((peers, chunks)),
             dma((peers, chunks)),
             dma((peers, chunks)),
             dma((peers, chunks)),
+            dma((ctx_size, chunks)),
+            dma((chunks,)),
         ],
         compiler_params=pltpu.CompilerParams(
-            collective_id=0, has_side_effects=True, vmem_limit_bytes=48 * 2**20
+            collective_id=0, has_side_effects=True, vmem_limit_bytes=62 * 2**20
         ),
     )(
         projected[0].transpose(1, 0, 2),

time: 43.5 us -> 37.1 us (0.85); the launches traced: 42.7 us -> 36.9 us
  local copies, waits for them, and re-layouts: 5.81 us -> 2.29 us
  Pallas kernels: 36.9 us -> 34.6 us
    unnamed x11 -> x1, local copies, waits for them, and re-layouts: 5.81 us -> 2.29 us
    pallas_call x1, Pallas kernels: 36.9 us -> 34.6 us  [on_device(): pl.pallas_call(functools.partial(mixer_kernel, ctx_size, dp_size), out_sh...]
where the time goes in v3:
time: 37.1 us; the launch traced here: 36.9 us
  Pallas kernels  34.6 us (93%)
  local copies, waits for them, and re-layouts  2.29 us (6%)
    pallas_call x1, Pallas kernels, on_device(): pl.pallas_call(functools.partial(mixer_kernel, ctx_size, dp_size), out_sh...  34.6 us
    unnamed x1, local copies, waits for them, and re-layouts  2.29 us

profile of v3, /device:TPU:0, one launch (start us, length us, event | category | flops | bytes accessed | tf_op | source)
XLA Modules:
  0.0 36.9 jit_solution(9092696625668419961)
XLA Ops:
  0.0 34.6 %shard_map.64 = bf16[128,4096]{1,0:T(8,128)(2,1)} custom-call(bf16[3,128,4096]{2,1,0:T(8,128)(2,1)} %bitcast.6, f32[3,3,1024]{2,1,0:T(4,128)} %taps_ref.1, bf16[64,1024]{1,0:T(8,128)(2,1)} %filter_ref.1, f32[1,1024]{1,0:T(1,128)} %bitcast.7, bf16[1024,512]{1,0:T(8,128)(2,1)} %constant.4.clone.forward_hbm, bf16[512,1024]{1,0:T(8,128)(2,1)} %constant.5.clone.backward_hbm), custom_call_target="tpu_custom_call" | custom-call | tf_op jit(solution)/shard_map/pallas_call | solution.py:549
  34.6 2.3 %copy.8 = bf16[1,128,4096]{2,1,0:T(8,128)(2,1)} copy(bf16[1,128,4096]{2,1,0:T(8,128)(2,1)} %bitcast.5) | data formatting | bytes 2097152

commit v4 on v3

--- a/solution.py
+++ b/solution.py
@@ -200,7 +200,8 @@
     skip_hbm,
     forward_hbm,
     backward_hbm,
-    out_hbm,
+    queries_hbm,
+    response_hbm,
     x_ref,
     skip_ref,
     forward_ref,
@@ -214,7 +215,6 @@
     filter_spec,
     prod_ref,
     response_slab,
-    response_in,
     queries,
     local_sem,
     taps_send,
@@ -231,6 +231,7 @@
     resp_recv,
     out_sem,
     filter_sem,
+    response_sem,
 ):
     kernel_size = taps_ref.shape[0]
     channels = taps_ref.shape[2]
@@ -399,10 +400,13 @@
             device_id_type=MESH,
         )
 
-    def response_copy(i, chunk):
+    def columns_of(owner, chunk):
+        return pl.ds(pl.multiple_of(owner * channels + chunk * CHUNK, CHUNK), CHUNK)
+
+    def response_copy(i, chunk, owner):
         return pltpu.make_async_remote_copy(
             src_ref=response_slab.at[chunk, position_rows(dests[i]), :],
-            dst_ref=response_in.at[i, chunk],
+            dst_ref=response_hbm.at[:, columns_of(owner, chunk)],
             send_sem=resp_send.at[i, chunk],
             recv_sem=resp_recv.at[i, chunk],
             device_id={"ctx": dests[i]},
@@ -431,11 +435,19 @@
 
     lax.fori_loop(1, chunks, push_chunk, 0)
 
+    def out_copy(owner, chunk):
+        return pltpu.make_async_copy(
+            queries.at[owner, chunk],
+            queries_hbm.at[:, columns_of(owner, chunk)],
+            out_sem.at[owner, chunk],
+        )
+
     def fill_queries(chunk, carry):
         forward_filter(2, chunk)
 
         def one_owner(owner, inner):
             queries[owner, chunk] = short_filter(0, owner, chunk).astype(jnp.bfloat16)
+            out_copy(owner, chunk).start()
             return inner
 
         return lax.fori_loop(0, ctx_size, one_owner, carry)
@@ -474,27 +486,22 @@
         direct = skip_ref[:, columns] * gated.astype(jnp.float32)
         response_slab[chunk] = (long_part + direct).astype(jnp.bfloat16)
         for i in range(len(offsets)):
-            response_copy(i, chunk).start()
-        mix_into(me, chunk, response_slab[chunk, position_rows(me), :])
+            response_copy(i, chunk, me).start()
+        own_response(chunk).start()
         return carry
 
-    def out_copy(owner, chunk):
-        columns = pl.ds(pl.multiple_of(owner * channels + chunk * CHUNK, CHUNK), CHUNK)
+    def own_response(chunk):
         return pltpu.make_async_copy(
-            queries.at[owner, chunk], out_hbm.at[:, columns], out_sem.at[owner, chunk]
-        )
-
-    def mix_into(owner, chunk, response):
-        mixed = queries[owner, chunk].astype(jnp.float32) * response.astype(jnp.float32)
-        queries[owner, chunk] = mixed.astype(jnp.bfloat16)
-        out_copy(owner, chunk).start()
+            response_slab.at[chunk, position_rows(me), :],
+            response_hbm.at[:, columns_of(me, chunk)],
+            response_sem.at[chunk],
+        )
 
     lax.fori_loop(0, chunks, convolve, 0)
 
     def finish(chunk, carry):
         for i in reversed(range(len(offsets))):
-            response_copy(i, chunk).wait_recv()
-            mix_into(sources[i], chunk, response_in[i, chunk])
+            response_copy(i, chunk, sources[i]).wait_recv()
         return carry
 
     lax.fori_loop(0, chunks, finish, 0)
@@ -502,7 +509,8 @@
     def drain(chunk, carry):
         for i in range(len(offsets)):
             gated_copy(i, chunk, me).wait_send()
-            response_copy(i, chunk).wait_send()
+            response_copy(i, chunk, me).wait_send()
+        own_response(chunk).wait()
         for owner in range(ctx_size):
             out_copy(owner, chunk).wait()
         yfil_copy(0, 0, own_filter(chunk), dp, chunk).wait_send()
@@ -546,11 +554,11 @@
     zsize = dp_size // 2
     hbm_spec = pl.BlockSpec(memory_space=pltpu.HBM)
     dma = pltpu.SemaphoreType.DMA
-    mixed = pl.pallas_call(
+    queries, response = pl.pallas_call(
         functools.partial(mixer_kernel, ctx_size, dp_size),
-        out_shape=jax.ShapeDtypeStruct((rows, width), jnp.bfloat16),
+        out_shape=[jax.ShapeDtypeStruct((rows, width), jnp.bfloat16)] * 2,
         in_specs=[hbm_spec] * 6,
-        out_specs=hbm_spec,
+        out_specs=[hbm_spec] * 2,
         scratch_shapes=[
             pltpu.VMEM((streams, rows, width), jnp.bfloat16),
             pltpu.VMEM((1, channels), jnp.float32),
@@ -565,7 +573,6 @@
             pltpu.VMEM((2 * length, CHUNK), jnp.float32),
             pltpu.VMEM((2 * length, CHUNK), jnp.bfloat16),
             pltpu.VMEM((chunks, length, CHUNK), jnp.bfloat16),
-            pltpu.VMEM((peers, chunks, rows, CHUNK), jnp.bfloat16),
             pltpu.VMEM((ctx_size, chunks, rows, CHUNK), jnp.bfloat16),
             dma((5,)),
             dma((peers,)),
@@ -582,6 +589,7 @@
             dma((peers, chunks)),
             dma((ctx_size, chunks)),
             dma((chunks,)),
+            dma((chunks,)),
         ],
         compiler_params=pltpu.CompilerParams(
             collective_id=0, has_side_effects=True, vmem_limit_bytes=62 * 2**20
@@ -594,7 +602,7 @@
         forward,
         backward,
     )
-    return mixed[None]
+    return combine_rows(queries, response)[None]
 
 
 def solution(mesh):

time: 37.1 us -> 37.2 us (level)
  other arithmetic: 0 us -> 2.76 us
  local copies, waits for them, and re-layouts: 2.29 us -> 0 us
    broadcast_in_dim x0 -> x1, other arithmetic: none -> 2.76 us  [on_device(): return combine_rows(queries, response)[None]]
    unnamed x1 -> x0, local copies, waits for them, and re-layouts: 2.29 us -> none
where the time goes in v4:
time: 37.2 us; the launch traced here: 37 us
  Pallas kernels  34.3 us (92%)
  other arithmetic  2.76 us (7%)
    pallas_call x1, Pallas kernels, on_device(): pl.pallas_call(functools.partial(mixer_kernel, ctx_size, dp_size), out_sh...  34.3 us
    broadcast_in_dim x1, other arithmetic, on_device(): return combine_rows(queries, response)[None]  2.76 us

profile of v4, /device:TPU:0, one launch (start us, length us, event | category | flops | bytes accessed | tf_op | source)
XLA Modules:
  0.0 37.0 jit_solution(16137968782709860041)
XLA Ops:
  0.0 34.3 %shard_map.64 = (bf16[128,4096]{1,0:T(8,128)(2,1)}, bf16[128,4096]{1,0:T(8,128)(2,1)}) custom-call(bf16[3,128,4096]{2,1,0:T(8,128)(2,1)} %bitcast.6, f32[3,3,1024]{2,1,0:T(4,128)} %taps_ref.1, bf16[64,1024]{1,0:T(8,128)(2,1)} %filter_ref.1, f32[1,1024]{1,0:T(1,128)} %bitcast.7, bf16[1024,512]{1,0:T(8,128)(2,1)} %constant.4.clone.forward_hbm, ...), custom_call_target="tpu_custom_call" | custom-call | tf_op jit(solution)/shard_map/pallas_call | solution.py:557
  34.3 2.8 %fusion = bf16[1,128,4096]{2,1,0:T(8,128)(2,1)} fusion(bf16[128,4096]{1,0:T(8,128)(2,1)} %get-tuple-element.8, bf16[128,4096]{1,0:T(8,128)(2,1)} %get-tuple-element.7), kind=kLoop, calls=%fused_computation.1 | loop fusion | flops 2097152 | bytes 3145728 | tf_op jit(solution)/shard_map/broadcast_in_dim | solution.py:605
